TPU v7x, 256 devices: a whole 4x4x8 slice. The times are simulated.
256 devices in a mesh: dp: 16 (over x, y), head: 16 (over z, core).
Axes of the slice: x: 4, y: 4, z: 8, core: 2. Of those that a mesh axis runs over, the one named last changes fastest.
Arguments:
- latents: bfloat16 [2048, 512], P('dp'), may hold values from -6 to 6
- targets: bfloat16 [2048, 32768], P('dp', 'head'), may hold values from -6 to 6
- kv_weight: bfloat16 [512, 32768], P(None, 'head'), may hold values from -0.25 to 0.25
- momentum: float32 [512, 16, 2048], P(None, 'head', 'dp'), may hold values from -120 to 120
Outputs:
- momentum_out: float32 [512, 16, 2048], P(None, 'head', 'dp')
- update: float32 [512, 16, 2048], P(None, 'head', 'dp')
All inputs are finite; a program needn't handle non-finite values.
Results may differ from a plain program's by a relative error of at most 0.0003.
The roundings to bfloat16 on the way count: a program that leaves them out, or rounds other values in their place, can miss the bound.
Values may be sent and summed in bfloat16 or wider, within the bound.
A program may use at most 64 MiB of HBM per device.

v0:
```python
import math
import jax
import jax.numpy as jnp
from jax import lax
from jax.sharding import PartitionSpec as P

C = 32768
ITERS = 2
decay_rate = 0.95
linear_coef = 3.4445
square_coef = -4.775
quint_coef = 2.0315
epsilon = 1e-07


def gram_total(iterate):
    local_gram = lax.dot_general(
        iterate, iterate, (((1,), (1,)), ((), ())), precision=lax.Precision.HIGHEST
    )
    return lax.psum(local_gram, ("dp", "head"))


def local(latents, targets, kv_weight, momentum):
    latent_width = momentum.shape[0]
    sub_width = momentum.shape[2]
    total_tokens = latents.shape[0] * lax.axis_size("dp")
    residual = (
        jnp.dot(latents, kv_weight, preferred_element_type=jnp.float32)
        - targets.astype(jnp.float32)
    ).astype(jnp.bfloat16)
    gradient = lax.psum_scatter(
        lax.dot_general(
            residual, latents, (((0,), (0,)), ((), ())), preferred_element_type=jnp.float32
        ),
        "dp",
        scatter_dimension=0,
        tiled=True,
    ).T
    gradient = gradient * (1.0 / math.sqrt(total_tokens))
    previous = momentum.reshape(latent_width, sub_width)
    momentum_new = decay_rate * previous + gradient
    nesterov = gradient + decay_rate * momentum_new
    squares = lax.psum(jnp.sum(nesterov * nesterov), ("dp", "head"))
    inverse = 1.0 / (jnp.sqrt(squares) + epsilon)
    iterate = nesterov * inverse
    gram_matrix = gram_total(iterate)
    for iteration in range(ITERS):
        if iteration > 0:
            gram_matrix = gram_total(iterate)
        polynomial = square_coef * gram_matrix + quint_coef * jnp.dot(
            gram_matrix, gram_matrix, precision=lax.Precision.HIGHEST
        )
        iterate = linear_coef * iterate + jnp.dot(
            polynomial, iterate, precision=lax.Precision.HIGHEST
        )
    update = iterate * math.sqrt(C)
    return (
        momentum_new.reshape(latent_width, 1, sub_width),
        update.reshape(latent_width, 1, sub_width),
    )


def solution(mesh):
    return jax.shard_map(
        local,
        mesh=mesh,
        in_specs=(P("dp", None), P("dp", "head"), P(None, "head"), P(None, "head", "dp")),
        out_specs=(P(None, "head", "dp"), P(None, "head", "dp")),
        check_vma=False,
    )
```

profile of v0, /device:TPU:2, one launch (start us, length us, event | category | flops | bytes accessed | tf_op | source)
XLA Modules:
  0.0 706.9 jit_solution(13692104984853528014)
XLA Ops:
  7.2 0.0 copy-start
  7.2 0.0 reduce-scatter.2.cloned.1.call-start
  7.2 1.5 copy-done
  8.8 4.0 fusion.3
  12.8 0.0 reduce-scatter.2.cloned.1.call-update
  12.8 0.0 all-reduce.3.cloned.1.call-start
  12.9 0.9 copy-done.2
  13.7 0.1 copy.6
  13.9 84.5 %reduce-scatter.2.cloned.1.call-done = f32[128,512]{1,0:T(8,128)} async-done(((f32[2048,512]{1,0:T(8,128)}), f32[128,512]{1,0:T(8,128)}) %reduce-scatter.2.cloned.1.call-update) | async-done | bytes 262160 | tf_op jit(solution)/shard_map/reduce_scatter | solution.py:31
  98.3 1.6 multiply_reduce_fusion
  99.9 73.7 %psum.21 = f32[]{:T(128)} all-reduce(f32[]{:T(128)} %get-tuple-element.4), channel_id=1, replica_groups=mesh['dp'=16,'head'=16] {'dp','head'}, use_global_device_ids=true, to_apply=%region_2.0 | all-reduce | flops 1 | bytes 8 | tf_op jit(solution)/shard_map/psum | solution.py:43
  174.3 3.1 fusion.7
  177.5 0.0 all-reduce.3.cloned.1.call-update
  177.5 0.0 all-reduce.5.cloned.1.call-start
  177.5 254.9 %all-reduce.3.cloned.1.call-done = f32[512,512]{1,0:T(8,128)} async-done(((f32[512,512]{1,0:T(8,128)}), f32[512,512]{1,0:T(8,128)}) %all-reduce.3.cloned.1.call-update) | async-done | bytes 1048592 | tf_op jit(solution)/shard_map/psum | solution.py:20
  432.5 3.9 fusion.2
  436.4 1.2 convolution_add_fusion.1
  437.6 2.1 fusion.13
  439.7 0.0 all-reduce.5.cloned.1.call-update
  439.7 0.8 copy.9
  440.6 253.9 %all-reduce.5.cloned.1.call-done = f32[512,512]{1,0:T(8,128)} async-done(((f32[512,512]{1,0:T(8,128)}), f32[512,512]{1,0:T(8,128)}) %all-reduce.5.cloned.1.call-update) | async-done | bytes 1048592 | tf_op jit(solution)/shard_map/psum | solution.py:20
  694.4 3.9 fusion.1
  698.3 1.2 fusion.5
  699.6 0.8 copy.10
  (3 shorter events, 0.0 us)
Async XLA Ops:
  7.2 1.6 copy-start
  7.2 91.1 %reduce-scatter.2.cloned.1.call-start = ((), (), s32[]{:S(2)}) async-start(), calls=%async_computation.1 | async-start | bytes 4456448 | tf_op jit(solution)/shard_map/reduce_scatter | solution.py:31
  12.8 0.9 copy-start.2
  12.8 419.7 %all-reduce.3.cloned.1.call-start = ((), (), s32[]{:S(2)}) async-start(), calls=%async_computation.2 | async-start | bytes 2097152 | tf_op jit(solution)/shard_map/psum | solution.py:20
  177.5 258.9 %copy-start.1 = (f32[128,512]{1,0:T(8,128)S(1)}, f32[128,512]{1,0:T(8,128)}, u32[]{:S(2)}) copy-start(f32[128,512]{1,0:T(8,128)} %reduce-scatter.2.cloned.1.call-done) | copy-start | bytes 786436
  177.5 516.9 %all-reduce.5.cloned.1.call-start = ((), (), s32[]{:S(2)}) async-start(), calls=%async_computation.3 | async-start | bytes 2097152 | tf_op jit(solution)/shard_map/psum | solution.py:20
Sparse Core Ops, SparseCore 0:
  12.9 85.3 reduce-scatter.1
  177.6 254.8 all-reduce.2
  439.9 254.5 all-reduce.4
where the time goes:
time: 707 us
  waiting for transfers between devices  593 us (84%)
  blocking collectives  73.7 us (10%)
  matrix products  19.5 us (3%)
  between operations  14.5 us (2%)
    psum x2, waiting for transfers between devices, gram_total(): return lax.psum(local_gram, ('dp', 'head'))  509 us
    reduce_scatter x1, waiting for transfers between devices, local(): lax.psum_scatter(lax.dot_general(residual, latents, (((0,), (0,)), ((), (...  84.5 us
    psum x1, blocking collectives, local(): squares = lax.psum(jnp.sum(nesterov * nesterov), ('dp', 'head'))  73.7 us
  transfers between devices with their start and end apart: 3, of which 3 were waited for; matrix products, arithmetic and copies ran while one was open for 0% of the time, Pallas kernels for 0%

commit v1 on v0

--- a/solution.py
+++ b/solution.py
@@ -13,11 +13,16 @@
 epsilon = 1e-07
 
 
+def one_after_other(value, axis_one, axis_two):
+    inner = lax.psum(value, axis_one)
+    return lax.psum(inner, axis_two)
+
+
 def gram_total(iterate):
     local_gram = lax.dot_general(
         iterate, iterate, (((1,), (1,)), ((), ())), precision=lax.Precision.HIGHEST
     )
-    return lax.psum(local_gram, ("dp", "head"))
+    return one_after_other(local_gram, "dp", "head")
 
 
 def local(latents, targets, kv_weight, momentum):

time: 707 us -> 618 us (0.87)
  waiting for transfers between devices: 593 us -> 503 us
    psum x2 -> x4, waiting for transfers between devices: 509 us -> 419 us  [the longest x2 226 us: one_after_other(): return lax.psum(inner, axis_two)]
  transfers between devices with their start and end apart: 3 -> 5, of which waited for: 3 -> 5; matrix products, arithmetic and copies ran while one was open for 0% -> 0% of each run, Pallas kernels for 0% -> 0%
where the time goes in v1:
time: 618 us; the launch traced here: 617 us
  waiting for transfers between devices  503 us (81%)
  blocking collectives  73.7 us (12%)
  matrix products  19.9 us (3%)
  between operations  14.6 us (2%)
    psum x2, waiting for transfers between devices, one_after_other(): return lax.psum(inner, axis_two)  226 us
    psum x2, waiting for transfers between devices, one_after_other(): inner = lax.psum(value, axis_one)  193 us
    reduce_scatter x1, waiting for transfers between devices, local(): lax.psum_scatter(lax.dot_general(residual, latents, (((0,), (0,)), ((), (...  84.5 us
    psum x1, blocking collectives, local(): squares = lax.psum(jnp.sum(nesterov * nesterov), ('dp', 'head'))  73.7 us
  transfers between devices with their start and end apart: 5, of which 5 were waited for; matrix products, arithmetic and copies ran while one was open for 0% of the time, Pallas kernels for 0%

profile of v1, /device:TPU:2, one launch (start us, length us, event | category | flops | bytes accessed | tf_op | source)
XLA Modules:
  0.0 617.3 jit_solution(1752516662442821504)
XLA Ops:
  7.2 0.0 reduce-scatter.2.cloned.1.call-start
  7.2 1.5 copy-done
  8.8 4.0 fusion.3
  12.8 0.0 all-reduce.5.cloned.1.call-start
  12.9 0.9 copy-done.2
  13.7 0.1 copy.6
  13.9 84.5 %reduce-scatter.2.cloned.1.call-done = f32[128,512]{1,0:T(8,128)} async-done(((f32[2048,512]{1,0:T(8,128)}), f32[128,512]{1,0:T(8,128)}) %reduce-scatter.2.cloned.1.call-update) | async-done | bytes 262160 | tf_op jit(solution)/shard_map/reduce_scatter | solution.py:36
  98.3 1.6 multiply_reduce_fusion
  99.9 73.7 %psum.35 = f32[]{:T(128)} all-reduce(f32[]{:T(128)} %get-tuple-element.4), channel_id=1, replica_groups=mesh['dp'=16,'head'=16] {'dp','head'}, use_global_device_ids=true, to_apply=%region_2.0 | all-reduce | flops 1 | bytes 8 | tf_op jit(solution)/shard_map/psum | solution.py:48
  174.3 3.1 fusion.7
  177.5 0.0 all-reduce.7.cloned.1.call-start
  177.5 95.6 %all-reduce.5.cloned.1.call-done = f32[512,512]{1,0:T(8,128)} async-done(((f32[512,512]{1,0:T(8,128)}), f32[512,512]{1,0:T(8,128)}) %all-reduce.5.cloned.1.call-update) | async-done | bytes 1048592 | tf_op jit(solution)/shard_map/psum | solution.py:17
  273.2 0.0 all-reduce.9.cloned.1.call-start
  273.2 113.5 %all-reduce.7.cloned.1.call-done = f32[512,512]{1,0:T(8,128)} async-done(((f32[512,512]{1,0:T(8,128)}), f32[512,512]{1,0:T(8,128)}) %all-reduce.7.cloned.1.call-update) | async-done | bytes 1048592 | tf_op jit(solution)/shard_map/psum | solution.py:18
  386.8 4.1 fusion.2
  390.9 1.2 convolution_add_fusion.1
  392.1 2.1 fusion.13
  394.2 0.0 all-reduce.11.cloned.1.call-start
  394.2 97.0 %all-reduce.9.cloned.1.call-done = f32[512,512]{1,0:T(8,128)} async-done(((f32[512,512]{1,0:T(8,128)}), f32[512,512]{1,0:T(8,128)}) %all-reduce.9.cloned.1.call-update) | async-done | bytes 1048592 | tf_op jit(solution)/shard_map/psum | solution.py:17
  491.3 0.8 copy.9
  492.1 112.4 %all-reduce.11.cloned.1.call-done = f32[512,512]{1,0:T(8,128)} async-done(((f32[512,512]{1,0:T(8,128)}), f32[512,512]{1,0:T(8,128)}) %all-reduce.11.cloned.1.call-update) | async-done | bytes 1048592 | tf_op jit(solution)/shard_map/psum | solution.py:18
  604.6 4.1 fusion.1
  608.7 1.2 fusion.5
  609.9 0.8 copy.10
  (9 shorter events, 0.1 us)
Async XLA Ops:
  7.2 1.6 copy-start
  7.2 91.1 %reduce-scatter.2.cloned.1.call-start = ((), (), s32[]{:S(2)}) async-start(), calls=%async_computation.1 | async-start | bytes 4456448 | tf_op jit(solution)/shard_map/reduce_scatter | solution.py:36
  12.8 0.9 copy-start.2
  12.8 260.4 %all-reduce.5.cloned.1.call-start = ((), (), s32[]{:S(2)}) async-start(), calls=%async_computation.2 | async-start | bytes 2097152 | tf_op jit(solution)/shard_map/psum | solution.py:17
  177.5 209.3 %all-reduce.7.cloned.1.call-start = ((), (), s32[]{:S(2)}) async-start(), calls=%async_computation.3 | async-start | bytes 2097152 | tf_op jit(solution)/shard_map/psum | solution.py:18
  273.2 117.7 %copy-start.1 = (f32[128,512]{1,0:T(8,128)S(1)}, f32[128,512]{1,0:T(8,128)}, u32[]{:S(2)}) copy-start(f32[128,512]{1,0:T(8,128)} %reduce-scatter.2.cloned.1.call-done) | copy-start | bytes 786436
  273.2 218.1 %all-reduce.9.cloned.1.call-start = ((), (), s32[]{:S(2)}) async-start(), calls=%async_computation.4 | async-start | bytes 2097152 | tf_op jit(solution)/shard_map/psum | solution.py:17
  394.2 210.4 %all-reduce.11.cloned.1.call-start = ((), (), s32[]{:S(2)}) async-start(), calls=%async_computation.5 | async-start | bytes 2097152 | tf_op jit(solution)/shard_map/psum | solution.py:18
Sparse Core Ops, SparseCore 0:
  12.9 85.3 reduce-scatter.1
  177.6 95.5 all-reduce.4
  275.6 111.0 all-reduce.6
  394.3 96.9 all-reduce.8
  493.5 111.0 all-reduce.10
